TPU v7x, 256 devices: a whole 4x4x8 slice. The times are simulated.
256 devices in a mesh: req: 64 (over x_lo, z, y), tp: 4 (over x_hi, core).
Axes of the slice: x: 4 (x_hi: 2, x_lo: 2; x = x_hi * 2 + x_lo), y: 4, z: 8, core: 2. Of those that a mesh axis runs over, the one named last changes fastest.
Arguments:
- hidden: bfloat16 [64, 512, 1280], P('req'), may hold values from -6 to 6
- membership: int32 [64], P('req'), may hold values from 0 to 3
- lengths: int32 [64], P('req'), may hold values from 8 to 512, as said below
- owners: int32 [4, 16], replicated, may hold values from 0 to 63, as said below
- prefix_cache: bfloat16 [4096, 20, 128], P('req', 'tp'), may hold values from -6 to 6
- w_query: bfloat16 [1280, 1280], P(None, 'tp'), may hold values from -0.25 to 0.25
- w_key: bfloat16 [1280, 1280], P(None, 'tp'), may hold values from -0.25 to 0.25
- w_value: bfloat16 [1280, 1280], P(None, 'tp'), may hold values from -0.15625 to 0.15625
- key_scale: float32 [20, 64], P('tp'), may hold values from 0.5 to 6
- w_out: bfloat16 [1280, 1280], P('tp'), may hold values from -0.15625 to 0.15625
- step_rates: float32 [1280], replicated, may hold values from 0.1 to 0.8
Outputs:
- layer_out: bfloat16 [64, 512, 1280], P('req', None, 'tp')
Inputs may be any that keep to these rules, and one draw needn't show every extreme that they name: `lengths`: every request has at least one suffix token; some request has length 512. `owners`: each cache slot appears exactly once in the table.
All inputs are finite; a program needn't handle non-finite values.
Results may differ from a plain program's by a relative error of at most 0.0085.
Values may be sent and summed in bfloat16 or wider, within the bound.
No kernel may reach another device: no remote copies, remote signals or barrier semaphores. Data moves between devices by JAX's collectives and lax.ppermute only.
A program may use at most 128 MiB of HBM per device.

v0:
```python
import math
import jax
import jax.numpy as jnp
from jax import lax
from jax.sharding import PartitionSpec as P


def normed(values):
    return values * lax.rsqrt(jnp.mean(values * values, axis=-1, keepdims=True) + 1e-06)


def scaled_keys(raw_keys, key_scale, head_size):
    return (normed(raw_keys.astype(jnp.float32)) * key_scale / math.sqrt(head_size)).astype(
        jnp.bfloat16
    )


def partial_attention(queries, key_rows, value_rows, visible):
    scores = jnp.einsum("qhd,khd->hqk", queries, key_rows, preferred_element_type=jnp.float32)
    masked = jnp.where(visible[None], scores, -1e30)
    row_peak = jnp.max(masked, axis=-1)
    weights = jnp.where(visible[None], jnp.exp(masked - row_peak[..., None]), 0.0)
    row_total = jnp.sum(weights, axis=-1)
    weighted = jnp.einsum(
        "hqk,khd->hqd", weights.astype(jnp.bfloat16), value_rows, preferred_element_type=jnp.float32
    )
    return (row_peak, row_total, weighted)


def combine(earlier, later_part):
    row_peak = jnp.maximum(earlier[0], later_part[0])
    scale_one = jnp.exp(earlier[0] - row_peak)
    scale_two = jnp.exp(later_part[0] - row_peak)
    return (
        row_peak,
        earlier[1] * scale_one + later_part[1] * scale_two,
        earlier[2] * scale_one[..., None] + later_part[2] * scale_two[..., None],
    )


def local(
    hidden,
    membership,
    lengths,
    owners,
    prefix_cache,
    w_query,
    w_key,
    w_value,
    key_scale,
    w_out,
    step_rates,
):
    req_count, suf_len, model_width = hidden.shape
    heads_here, head_size = key_scale.shape
    row_count = req_count * suf_len
    flat_rows = hidden.reshape(row_count, model_width)
    queries = (
        normed(
            jnp.dot(flat_rows, w_query, preferred_element_type=jnp.float32).reshape(
                req_count, suf_len, heads_here, head_size
            )
        )
        * key_scale
    ).astype(jnp.bfloat16)
    key_rows = scaled_keys(
        jnp.dot(flat_rows, w_key, preferred_element_type=jnp.float32).reshape(
            req_count, suf_len, heads_here, head_size
        ),
        key_scale,
        head_size,
    )
    value_rows = (
        jnp.dot(flat_rows, w_value, preferred_element_type=jnp.float32)
        .astype(jnp.bfloat16)
        .reshape(req_count, suf_len, heads_here, head_size)
    )
    positions = jnp.arange(suf_len)
    causal = positions[None, :] <= positions[:, None]

    def local_attention(inputs):
        query_one, keys_one, values_one, length_one = inputs
        return partial_attention(
            query_one, keys_one, values_one, causal & (positions[None, :] < length_one)
        )

    local_part = lax.map(local_attention, (queries, key_rows, value_rows, lengths))
    slot_rows = prefix_cache.shape[0]
    gathered = lax.all_gather(prefix_cache, "req", axis=0, tiled=True)
    slot_table = gathered.reshape(-1, slot_rows, heads_here, 2 * head_size)[owners]
    slot_table = slot_table.reshape(owners.shape[0], -1, heads_here, 2 * head_size)
    pre_keys = scaled_keys(slot_table[..., :head_size], key_scale, head_size)
    pre_values = slot_table[..., head_size:]
    everyone = jnp.ones((1, pre_keys.shape[1]), bool)

    def prefix_attention(inputs):
        query_one, group_one = inputs
        return partial_attention(query_one, pre_keys[group_one], pre_values[group_one], everyone)

    prefix_part = lax.map(prefix_attention, (queries, membership))
    merged = combine(prefix_part, local_part)
    attended = merged[2] / merged[1][..., None]
    attended = (
        attended.transpose(0, 2, 1, 3)
        .reshape(row_count, heads_here * head_size)
        .astype(jnp.bfloat16)
    )
    partial_out = jnp.dot(attended, w_out, preferred_element_type=jnp.float32)
    valid = (positions[None, :] < lengths[:, None]).reshape(row_count, 1)
    part_width = model_width // lax.axis_size("tp")
    offset = lax.axis_index("tp") * part_width
    summed = lax.psum(partial_out.astype(jnp.bfloat16), "tp").astype(jnp.float32)
    branch = normed(summed)
    state_rows = flat_rows.astype(jnp.float32)
    updated = normed(state_rows + step_rates * (branch - state_rows))
    result = lax.dynamic_slice_in_dim(updated, offset, part_width, 1)
    layer_out = jnp.where(valid, result, 0.0).astype(jnp.bfloat16)
    return layer_out.reshape(req_count, suf_len, part_width)


def solution(mesh):
    in_specs = (
        P("req", None, None),
        P("req"),
        P("req"),
        P(),
        P("req", "tp", None),
        P(None, "tp"),
        P(None, "tp"),
        P(None, "tp"),
        P("tp", None),
        P("tp", None),
        P(),
    )
    out_specs = P("req", None, "tp")
    return jax.shard_map(local, mesh=mesh, in_specs=in_specs, out_specs=out_specs, check_vma=False)
```

profile of v0, /device:TPU:1, one launch (start us, length us, event | category | flops | bytes accessed | tf_op | source)
XLA Modules:
  0.0 428.9 jit_solution(8274242587962377966)
XLA Ops:
  6.5 0.7 all-gather.2.cloned.1.call-update
  7.3 0.0 all-reduce.2.cloned.1.call-start
  7.3 0.7 compare_select_fusion
  8.0 0.1 reshape.221
  8.7 0.0 copy-start.3
  8.7 3.0 fusion.69
  11.8 0.1 reduce_sum.67
  11.8 2.2 fusion.67
  14.0 0.1 reduce_sum.65
  14.8 0.1 fusion.43
  14.9 1.8 fusion.40
  16.7 2.3 select_reduce_fusion
  19.0 2.4 copy-done.1
  21.4 1.1 fusion.5
  22.5 251.3 %all-gather.2.cloned.1.call-done = bf16[4096,5,128]{2,0,1:T(8,128)(2,1)} async-done(((bf16[64,5,128]{2,0,1:T(8,128)(2,1)}), bf16[4096,5,128]{2,0,1:T(8,128)(2,1)}) %all-gather.2.cloned.1.call-update) | async-done | bytes 5242896 | tf_op jit(solution)/shard_map/all_gather | solution.py:89
  273.8 6.1 %copy.23 = bf16[64,64,5,128]{3,1,2,0:T(8,128)(2,1)} copy(bf16[64,64,5,128]{3,1,0,2:T(8,128)(2,1)} %bitcast.59) | data formatting | bytes 10485760 | tf_op jit(solution)/shard_map/reshape | solution.py:90
  279.9 6.0 %gather_fusion = bf16[64,64,5,128]{3,1,2,0:T(8,128)(2,1)} fusion(bf16[64,64,5,128]{3,1,2,0:T(8,128)(2,1)} %copy.23, s32[1024]{0:T(1024)S(1)} %pad_clamp_fusion), kind=kCustom, calls=%fused_computation | custom fusion | bytes 10486016 | tf_op jit(solution)/shard_map/gather | solution.py:90
  285.9 6.4 %copy.24 = bf16[64,64,5,128]{3,1,0,2:T(8,128)(2,1)} copy(bf16[64,64,5,128]{3,1,2,0:T(8,128)(2,1)} %gather_fusion) | data formatting | bytes 10485760 | tf_op jit(solution)/shard_map/gather | solution.py:90
  292.4 11.2 %slice_convert_fusion = (f32[4,1024,5,64]{3,1,0,2:T(8,128)}, bf16[4,1024,5,64]{3,1,0,2:T(8,128)(2,1)}) fusion(bf16[4,1024,5,128]{3,1,0,2:T(8,128)(2,1)} %bitcast.53), kind=kLoop, calls=%fused_computation.6 | loop fusion | flops 1310720 | bytes 13107200 | tf_op jit(solution)/shard_map/convert_element_type | solution.py:13
  303.5 5.5 %multiply_reduce_fusion = f32[4,1024,5]{1,0,2:T(4,128)S(1)} fusion(bf16[4,1024,5,128]{3,1,0,2:T(8,128)(2,1)} %bitcast.54), kind=kLoop, calls=%fused_computation.2 | loop fusion | flops 3911680 | bytes 2703360 | tf_op jit(solution)/shard_map/reduce_sum | solution.py:9
  309.1 4.0 fusion.68
  313.1 2.3 fusion
  315.4 3.3 fusion.35
  318.7 0.0 copy-start.4
  318.7 1.6 fusion.47
  320.3 2.0 convolution_convert_fusion
  322.2 0.0 all-reduce.2.cloned.1.call-update
  322.3 94.6 %all-reduce.2.cloned.1.call-done = bf16[512,1280]{1,0:T(8,128)(2,1)} async-done(((bf16[512,1280]{1,0:T(8,128)(2,1)}), bf16[512,1280]{1,0:T(8,128)(2,1)}) %all-reduce.2.cloned.1.call-update) | async-done | bytes 1310736 | tf_op jit(solution)/shard_map/psum | solution.py:112
  416.8 1.6 fusion.8
  418.5 2.2 multiply_reduce_fusion.1
  420.7 0.4 fusion.52
  421.2 0.9 copy.28
  (21 shorter events, 0.1 us)
Async XLA Ops:
  6.5 313.8 %copy-start = (bf16[320,1280]{1,0:T(8,128)(2,1)S(1)}, bf16[320,1280]{1,0:T(8,128)(2,1)}, u32[]{:S(2)}) copy-start(bf16[320,1280]{1,0:T(8,128)(2,1)} %param.20) | copy-start | bytes 2457604
  6.5 8.4 %copy-start.2 = (bf16[1,512,1280]{2,1,0:T(8,128)(2,1)S(1)}, bf16[1,512,1280]{2,1,0:T(8,128)(2,1)}, u32[]{:S(2)}) copy-start(bf16[1,512,1280]{2,1,0:T(8,128)(2,1)} %param.11) | copy-start | bytes 3932164
  6.5 267.3 %all-gather.2.cloned.1.call-start = ((), (), s32[]{:S(2)}) async-start(), calls=%async_computation | async-start | bytes 5324800 | tf_op jit(solution)/shard_map/all_gather | solution.py:89
  7.3 409.6 %all-reduce.2.cloned.1.call-start = ((), (), s32[]{:S(2)}) async-start(), calls=%async_computation.1 | async-start | bytes 2621440 | tf_op jit(solution)/shard_map/psum | solution.py:112
  8.7 8.0 %copy-start.3 = (f32[5,64]{1,0:T(8,128)S(1)}, f32[5,64]{1,0:T(8,128)}, u32[]{:S(2)}) copy-start(f32[5,64]{1,0:T(8,128)} %param.19) | copy-start | bytes 3844
  19.0 2.4 copy-start.1
  313.0 5.6 %slice-start = ((s8[5242880]{0:T(1024)(128)(4,1)}), s8[4194304]{0:T(1024)(128)(4,1)S(1)}, s32[]{:S(2)}) async-start(s8[5242880]{0:T(1024)(128)(4,1)} %bitcast.55), calls=%async_computation.2 | async-start | bytes 8388608
  315.4 3.3 slice-start.1
  318.7 99.8 %copy-start.4 = (f32[1280]{0:T(1024)S(1)}, f32[1280]{0:T(1024)}, u32[]{:S(2)}) copy-start(f32[1280]{0:T(1024)} %param.21) | copy-start | bytes 15364
Sparse Core Ops, SparseCore 0:
  9.1 264.6 all-gather.1
  322.4 94.4 all-reduce.1
where the time goes:
time: 429 us
  waiting for transfers between devices  347 us (81%)
  other arithmetic  25.3 us (6%)
  local copies, waits for them, and re-layouts  21.9 us (5%)
  matrix products  20 us (5%)
  between operations  14.9 us (3%)
    all_gather x1, waiting for transfers between devices, local(): gathered = lax.all_gather(prefix_cache, 'req', axis=0, tiled=True)  251 us
    psum x1, waiting for transfers between devices, local(): lax.psum(partial_out.astype(jnp.bfloat16), 'tp').astype(jnp.float32)  94.6 us
    gather x2, local copies, waits for them, and re-layouts, local(): gathered.reshape(-1, slot_rows, heads_here, 2 * head_size)[owners]  12.4 us
    convert_element_type x1, other arithmetic, scaled_keys(): raw_keys.astype(jnp.float32)  11.2 us
    reduce_sum x5, other arithmetic, normed(): jnp.mean(values * values, axis=-1, keepdims=True) + 1e-06  9.4 us
  transfers between devices with their start and end apart: 2, of which 2 were waited for; matrix products, arithmetic and copies ran while one was open for 3% of the time, Pallas kernels for 0%

commit v1 on v0

--- a/solution.py
+++ b/solution.py
@@ -86,7 +86,9 @@
 
     local_part = lax.map(local_attention, (queries, key_rows, value_rows, lengths))
     slot_rows = prefix_cache.shape[0]
-    gathered = lax.all_gather(prefix_cache, "req", axis=0, tiled=True)
+    gathered = jnp.concatenate(
+        lax.all_to_all(jnp.stack([prefix_cache] * lax.axis_size("req"), 0), "req", 0, 0), 0
+    )
     slot_table = gathered.reshape(-1, slot_rows, heads_here, 2 * head_size)[owners]
     slot_table = slot_table.reshape(owners.shape[0], -1, heads_here, 2 * head_size)
     pre_keys = scaled_keys(slot_table[..., :head_size], key_scale, head_size)

time: 429 us -> 248 us (0.58)
  waiting for transfers between devices: 347 us -> 154 us
  starting transfers between devices: 0.04 us -> 14 us
    all_gather x1 -> x0, waiting for transfers between devices: 251 us -> none  [local(): gathered = lax.all_gather(prefix_cache, 'req', axis=0, tiled=True)]
    all_to_all x0 -> x1, waiting for transfers between devices: none -> 102 us  [local(): lax.all_to_all(jnp.stack([prefix_cache] * lax.axis_size('req'), 0), 'req'...]
    psum x1, waiting for transfers between devices: 94.6 us -> 52.6 us  [local(): lax.psum(partial_out.astype(jnp.bfloat16), 'tp').astype(jnp.float32)]
    all_to_all x0 -> x1, starting transfers between devices: none -> 13.9 us  [local(): lax.all_to_all(jnp.stack([prefix_cache] * lax.axis_size('req'), 0), 'req'...]
    reshape x1 -> x0, local copies, waits for them, and re-layouts: 6.08 us -> none  [local(): gathered.reshape(-1, slot_rows, heads_here, 2 * head_size)[owners]]
    another operation x0 -> x1, local copies, waits for them, and re-layouts: none -> 4.65 us  [local(): jnp.stack([prefix_cache] * lax.axis_size('req'), 0)]
  transfers between devices with their start and end apart: 2 -> 2, of which waited for: 2 -> 2; matrix products, arithmetic and copies ran while one was open for 3% -> 4% of each run, Pallas kernels for 0% -> 0%
where the time goes in v1:
time: 248 us
  waiting for transfers between devices  154 us (62%)
  other arithmetic  24.5 us (10%)
  local copies, waits for them, and re-layouts  20.5 us (8%)
  matrix products  19.4 us (8%)
  between operations  15 us (6%)
  starting transfers between devices  14 us (6%)
    all_to_all x1, waiting for transfers between devices, local(): lax.all_to_all(jnp.stack([prefix_cache] * lax.axis_size('req'), 0), 'req'...  102 us
    psum x1, waiting for transfers between devices, local(): lax.psum(partial_out.astype(jnp.bfloat16), 'tp').astype(jnp.float32)  52.6 us
    all_to_all x1, starting transfers between devices, local(): lax.all_to_all(jnp.stack([prefix_cache] * lax.axis_size('req'), 0), 'req'...  13.9 us
    gather x2, local copies, waits for them, and re-layouts, local(): gathered.reshape(-1, slot_rows, heads_here, 2 * head_size)[owners]  12.5 us
    convert_element_type x1, other arithmetic, scaled_keys(): raw_keys.astype(jnp.float32)  11.2 us
    reduce_sum x5, other arithmetic, normed(): jnp.mean(values * values, axis=-1, keepdims=True) + 1e-06  9.22 us
    dot_general x2, matrix products, partial_attention(): jnp.einsum('qhd,khd->hqk', queries, key_rows, preferred_element_type=jnp....  6.47 us
  transfers between devices with their start and end apart: 2, of which 2 were waited for; matrix products, arithmetic and copies ran while one was open for 4% of the time, Pallas kernels for 0%

profile of v1, /device:TPU:1, one launch (start us, length us, event | category | flops | bytes accessed | tf_op | source)
XLA Modules:
  0.0 247.7 jit_solution(14314030911828907827)
XLA Ops:
  6.5 4.6 %stack.2 = bf16[64,64,5,128]{3,1,2,0:T(8,128)(2,1)} broadcast(bf16[64,5,128]{2,0,1:T(8,128)(2,1)} %param.15), dimensions={1,2,3} | broadcast | bytes 5324800 | tf_op jit(solution)/shard_map/stack | solution.py:90
  11.2 13.9 %all-to-all-start = ((bf16[64,64,5,128]{3,1,2,0:T(8,128)(2,1)}), bf16[64,64,5,128]{3,1,2,0:T(8,128)(2,1)}, u32[]{:S(2)}, u32[]{:S(2)}) async-start(bf16[64,64,5,128]{3,1,2,0:T(8,128)(2,1)} %stack.2), calls=%async_computation | async-start | bytes 10485760 | tf_op jit(solution)/shard_map/all_to_all | solution.py:90
  25.1 0.0 all-reduce.2.cloned.1.call-start
  25.2 0.1 reshape.219
  25.9 0.0 copy-start.3
  26.0 2.6 %fusion.69 = (f32[512,320]{0,1:T(8,128)S(1)}, f32[512,320]{0,1:T(8,128)}) fusion(bf16[1280,320]{0,1:T(8,128)(2,1)} %param.17, bf16[1,512,1280]{2,1,0:T(8,128)(2,1)S(1)} %copy-done.2), kind=kOutput, calls=%fused_computation.79 | convolution fusion | flops 419594240 | bytes 3440640 | tf_op jit(solution)/shard_map/dot_general | solution.py:67
  28.6 0.1 reduce_sum.67
  28.7 1.8 fusion.67
  30.4 0.1 reduce_sum.65
  31.2 0.1 fusion.43
  31.3 1.8 fusion.40
  33.1 2.3 select_reduce_fusion
  35.5 2.4 copy-done.1
  37.8 1.1 fusion.5
  38.9 101.7 %all-to-all-done = bf16[64,64,5,128]{3,1,2,0:T(8,128)(2,1)} async-done(((bf16[64,64,5,128]{3,1,2,0:T(8,128)(2,1)}), bf16[64,64,5,128]{3,1,2,0:T(8,128)(2,1)}, u32[]{:S(2)}, u32[]{:S(2)}) %all-to-all-start) | async-done | bytes 5242912 | tf_op jit(solution)/shard_map/all_to_all | solution.py:90
  140.6 6.1 %gather_fusion = bf16[64,64,5,128]{3,1,2,0:T(8,128)(2,1)} fusion(bf16[64,64,5,128]{3,1,2,0:T(8,128)(2,1)} %all-to-all-done, s32[1024]{0:T(1024)S(1)} %pad_clamp_fusion), kind=kCustom, calls=%fused_computation | custom fusion | bytes 10486016 | tf_op jit(solution)/shard_map/gather | solution.py:92
  146.7 6.4 %copy.20 = bf16[64,64,5,128]{3,1,0,2:T(8,128)(2,1)} copy(bf16[64,64,5,128]{3,1,2,0:T(8,128)(2,1)} %gather_fusion) | data formatting | bytes 10485760 | tf_op jit(solution)/shard_map/gather | solution.py:92
  153.1 11.2 %slice_convert_fusion = (f32[4,1024,5,64]{3,1,0,2:T(8,128)}, bf16[4,1024,5,64]{3,1,0,2:T(8,128)(2,1)}) fusion(bf16[4,1024,5,128]{3,1,0,2:T(8,128)(2,1)} %bitcast.52), kind=kLoop, calls=%fused_computation.6 | loop fusion | flops 1310720 | bytes 13107200 | tf_op jit(solution)/shard_map/convert_element_type | solution.py:13
  164.3 5.3 %multiply_reduce_fusion = f32[4,1024,5]{1,0,2:T(4,128)S(1)} fusion(bf16[4,1024,5,128]{3,1,0,2:T(8,128)(2,1)} %bitcast.53), kind=kLoop, calls=%fused_computation.2 | loop fusion | flops 3911680 | bytes 2703360 | tf_op jit(solution)/shard_map/reduce_sum | solution.py:9
  169.6 4.1 %fusion.68 = (f32[5,512]{1,0:T(8,128)S(1)}, f32[5,512,1024]{2,1,0:T(8,128)S(1)}) fusion(f32[4,1024,5,64]{3,1,0,2:T(8,128)} %get-tuple-element.46, s32[]{:T(128)S(6)} %select_n.30, f32[5,64]{1,0:T(8,128)S(1)} %copy-done.3, f32[1,1024,5]{1,0,2:T(1,128)S(1)} %constant_dynamic-slice_fusion, f32[512,5,64]{0,2,1:T(8,128)S(1)} %bitcast.57, ...), kind=kOutput, calls=%fused_computation.78 | convolution fusion | flops 339965440 | bytes 13817860 | tf_op jit(solution)/shard_map/while/body/eval_jaxpr/qhd,khd->hqk/dot_general | solution.py:19
  173.8 0.0 slice-start
  173.8 2.3 fusion
  176.1 3.3 %fusion.35 = f32[5,512,64]{1,2,0:T(8,128)S(1)} fusion(bf16[4,1024,5,64]{3,1,0,2:T(8,128)(2,1)} %get-tuple-element.47, s32[]{:T(128)S(6)} %select_n.30, f32[5,512,1024]{2,1,0:T(8,128)S(1)} %get-tuple-element.59, f32[5,512]{1,0:T(8,128)S(1)} %get-tuple-element.58, f32[5,512]{1,0:T(8,128)S(1)} %get-tuple-element.45), kind=kOutput, calls=%fused_computation.41 | convolution fusion | flops 340951040 | bytes 12472324 | tf_op jit(solution)/shard_map/while/body/eval_jaxpr/hqk,khd->hqd/dot_general | solution.py:24
  179.4 0.0 copy-start.4
  179.4 1.6 fusion.47
  181.0 2.0 convolution_convert_fusion
  183.0 0.0 all-reduce.2.cloned.1.call-update
  183.0 52.6 %all-reduce.2.cloned.1.call-done = bf16[512,1280]{1,0:T(8,128)(2,1)} async-done(((bf16[512,1280]{1,0:T(8,128)(2,1)}), bf16[512,1280]{1,0:T(8,128)(2,1)}) %all-reduce.2.cloned.1.call-update) | async-done | bytes 1310736 | tf_op jit(solution)/shard_map/psum | solution.py:114
  235.6 1.6 fusion.8
  237.3 2.2 multiply_reduce_fusion.1
  239.5 0.4 fusion.52
  239.9 0.9 copy.24
  (22 shorter events, 0.1 us)
Async XLA Ops:
  6.5 174.5 %copy-start = (bf16[320,1280]{1,0:T(8,128)(2,1)S(1)}, bf16[320,1280]{1,0:T(8,128)(2,1)}, u32[]{:S(2)}) copy-start(bf16[320,1280]{1,0:T(8,128)(2,1)} %param.20) | copy-start | bytes 2457604
  11.2 14.0 %copy-start.5 = (s32[4,16]{1,0:T(4,128)S(1)}, s32[4,16]{1,0:T(4,128)}, u32[]{:S(2)}) copy-start(s32[4,16]{1,0:T(4,128)} %param.14) | copy-start | bytes 772
  11.2 14.8 %copy-start.2 = (bf16[1,512,1280]{2,1,0:T(8,128)(2,1)S(1)}, bf16[1,512,1280]{2,1,0:T(8,128)(2,1)}, u32[]{:S(2)}) copy-start(bf16[1,512,1280]{2,1,0:T(8,128)(2,1)} %param.11) | copy-start | bytes 3932164
  11.2 129.4 %all-to-all-start = ((bf16[64,64,5,128]{3,1,2,0:T(8,128)(2,1)}), bf16[64,64,5,128]{3,1,2,0:T(8,128)(2,1)}, u32[]{:S(2)}, u32[]{:S(2)}) async-start(bf16[64,64,5,128]{3,1,2,0:T(8,128)(2,1)} %stack.2), calls=%async_computation | async-start | bytes 10485760 | tf_op jit(solution)/shard_map/all_to_all | solution.py:90
  25.1 210.5 %all-reduce.2.cloned.1.call-start = ((), (), s32[]{:S(2)}) async-start(), calls=%async_computation.1 | async-start | bytes 2621440 | tf_op jit(solution)/shard_map/psum | solution.py:114
  25.9 7.2 %copy-start.3 = (f32[5,64]{1,0:T(8,128)S(1)}, f32[5,64]{1,0:T(8,128)}, u32[]{:S(2)}) copy-start(f32[5,64]{1,0:T(8,128)} %param.19) | copy-start | bytes 3844
  35.5 2.4 copy-start.1
  173.8 5.6 %slice-start = ((s8[5242880]{0:T(1024)(128)(4,1)}), s8[4194304]{0:T(1024)(128)(4,1)S(1)}, s32[]{:S(2)}) async-start(s8[5242880]{0:T(1024)(128)(4,1)} %bitcast.54), calls=%async_computation.2 | async-start | bytes 8388608
  176.1 3.3 %slice-start.1 = ((s8[5242880]{0:T(1024)(128)(4,1)}), s8[1048576]{0:T(1024)(128)(4,1)S(1)}, s32[]{:S(2)}) async-start(s8[5242880]{0:T(1024)(128)(4,1)} %bitcast.54), calls=%async_computation.3 | async-start | bytes 2097152
  179.4 57.9 %copy-start.4 = (f32[1280]{0:T(1024)S(1)}, f32[1280]{0:T(1024)}, u32[]{:S(2)}) copy-start(f32[1280]{0:T(1024)} %param.21) | copy-start | bytes 15364
Sparse Core Ops, SparseCore 0:
  183.1 52.4 all-reduce.1
